TPU v7x, 32 devices: a whole 2x2x4 slice. The times are simulated.
32 devices in a mesh: section: 2 (over core), dp: 8 (over z, x), rep: 2 (over y).
Axes of the slice: x: 2, y: 2, z: 4, core: 2. Of those that a mesh axis runs over, the one named last changes fastest.
Arguments:
- inputs: bfloat16 [4096, 1024], P(('dp', 'rep')), may hold values from -6 to 6
- cotangent: bfloat16 [4096, 1024], P(('dp', 'rep')), may hold values from -6 to 6
- seg_counts: int32 [256], P(('dp', 'rep')), may hold values from 2 to 16
- w_qkv: bfloat16 [2, 1024, 3072], P('section'), may hold values from -0.1875 to 0.1875
- w_out: bfloat16 [2, 1024, 1024], P('section'), may hold values from -0.375 to 0.375
- w_up: bfloat16 [2, 1024, 2048], P('section'), may hold values from -0.1875 to 0.1875
- w_down: bfloat16 [2, 2048, 1024], P('section'), may hold values from -0.1875 to 0.1875
- gains: float32 [2, 2, 1024], P('section'), may hold values from 0.5 to 1.5
- biases: float32 [2, 2, 1024], P('section'), may hold values from -3 to 3
Outputs:
- layer_outputs: bfloat16 [2, 4096, 1024], P('section', ('dp', 'rep'))
- input_grads: bfloat16 [2, 4096, 1024], P('section', ('dp', 'rep'))
- grad_qkv: float32 [2, 1024, 3072], P('section', 'dp')
- grad_wout: float32 [2, 1024, 1024], P('section', None, 'dp')
- grad_up: float32 [2, 1024, 2048], P('section', 'dp')
- grad_down: float32 [2, 2048, 1024], P('section', None, 'dp')
- grad_gains: float32 [2, 2, 1024], P('section', None, 'dp')
- grad_biases: float32 [2, 2, 1024], P('section', None, 'dp')
Inputs may be any that keep to these rules, and one draw needn't show every extreme that they name: seg_counts gives each series' number of valid slots; the first 16 - seg_counts slots of a series are padding.
All inputs are finite; a program needn't handle non-finite values.
Results may differ from a plain program's by a relative error of at most 0.015.
Values may be sent and summed in bfloat16 or wider, within the bound.
A program may use at most 256 MiB of HBM per device.

v0:
```python
from functools import partial

import jax
import jax.numpy as jnp
from jax import lax
from jax.sharding import PartitionSpec as P

SEG = 16
MB_SER = 8
HEAD_DIM = 128


epsilon = 1e-05


def from_behind(block, axis, distance):
    devices = range(lax.axis_size(axis))
    route = [(i - distance, i) for i in devices if i - distance in devices]
    return lax.ppermute(block, axis, route)


def normalize(hidden):
    average = jnp.mean(hidden, axis=-1, keepdims=True)
    centred = hidden - average
    inverse = lax.rsqrt(jnp.mean(centred * centred, axis=-1, keepdims=True) + epsilon)
    return (centred * inverse, inverse)


def normalize_back(grad_normed, normed, inverse):
    centre_term = jnp.mean(grad_normed, axis=-1, keepdims=True)
    slope_term = normed * jnp.mean(grad_normed * normed, axis=-1, keepdims=True)
    return inverse * (grad_normed - centre_term - slope_term)


def allowed_pairs(counts):
    number = counts.shape[0]
    rows = number * SEG
    position = jnp.broadcast_to(jnp.arange(SEG, dtype=jnp.int32)[None, :], (number, SEG)).reshape(
        rows
    )
    first = jnp.broadcast_to((SEG - counts)[:, None], (number, SEG)).reshape(rows)
    owner = jnp.broadcast_to(jnp.arange(number, dtype=jnp.int32)[:, None], (number, SEG)).reshape(
        rows
    )
    row_ids = jnp.arange(rows, dtype=jnp.int32)
    same_series = owner[:, None] == owner[None, :]
    causal = position[None, :] <= position[:, None]
    valid = (position >= first)[None, :] | (row_ids[:, None] == row_ids[None, :])
    return same_series & causal & valid


def probabilities(queries, keys_in, allowed):
    scores = jnp.einsum(
        "qhd,khd->hqk", queries, keys_in, preferred_element_type=jnp.float32
    ) * HEAD_DIM ** (-0.5)
    scores = jnp.where(allowed[None], scores, -1e30)
    largest = jnp.max(scores, axis=-1, keepdims=True)
    raised = jnp.exp(scores - largest)
    return raised / jnp.sum(raised, axis=-1, keepdims=True)


def keep_local(value):
    return value


def layer_forward(hidden_b, params, allowed, joins):
    w_qkv, w_out, w_up, w_down, gains, biases = params
    attention_join, feed_join = (joins[0], joins[1])
    rows = hidden_b.shape[0]
    local_heads = w_qkv.shape[1] // (3 * HEAD_DIM)
    hidden = hidden_b.astype(jnp.float32)
    normed_one, inverse_one = normalize(hidden)
    first_b = (normed_one * gains[0] + biases[0]).astype(jnp.bfloat16)
    packed_b = jnp.dot(first_b, w_qkv, preferred_element_type=jnp.float32).astype(jnp.bfloat16)
    split = packed_b.reshape(rows, 3, local_heads, HEAD_DIM)
    probs = probabilities(split[:, 0], split[:, 1], allowed)
    probs_b = probs.astype(jnp.bfloat16)
    mixed = jnp.einsum("hqk,khd->qhd", probs_b, split[:, 2], preferred_element_type=jnp.float32)
    mixed_b = mixed.reshape(rows, local_heads * HEAD_DIM).astype(jnp.bfloat16)
    middle = hidden + attention_join(jnp.dot(mixed_b, w_out, preferred_element_type=jnp.float32))
    normed_two, inverse_two = normalize(middle)
    second_b = (normed_two * gains[1] + biases[1]).astype(jnp.bfloat16)
    upper = jnp.dot(second_b, w_up, preferred_element_type=jnp.float32)
    active_b = jax.nn.gelu(upper, approximate=True).astype(jnp.bfloat16)
    result_b = (
        middle + feed_join(jnp.dot(active_b, w_down, preferred_element_type=jnp.float32))
    ).astype(jnp.bfloat16)
    saved = (
        normed_one,
        inverse_one,
        first_b,
        split,
        probs,
        probs_b,
        mixed_b,
        normed_two,
        inverse_two,
        second_b,
        upper,
        active_b,
    )
    return (result_b, saved)


def layer_backward(hidden_b, grad_b, params, allowed, joins):
    w_qkv, w_out, w_up, w_down, gains, biases = params
    feed_back, attention_back = (joins[2], joins[3])
    rows = hidden_b.shape[0]
    local_heads = w_qkv.shape[1] // (3 * HEAD_DIM)
    saved = layer_forward(hidden_b, params, allowed, joins)[1]
    (
        normed_one,
        inverse_one,
        first_b,
        split,
        probs,
        probs_b,
        mixed_b,
        normed_two,
        inverse_two,
        second_b,
        upper,
        active_b,
    ) = saved
    grad_result = grad_b.astype(jnp.float32)
    grad_down = jnp.einsum("rf,rd->fd", active_b, grad_b, preferred_element_type=jnp.float32)
    grad_active = jnp.einsum("rd,fd->rf", grad_b, w_down, preferred_element_type=jnp.float32)
    grad_upper = jax.vjp(partial(jax.nn.gelu, approximate=True), upper)[1](grad_active)[0]
    grad_upper_b = grad_upper.astype(jnp.bfloat16)
    grad_up = jnp.einsum("rd,rf->df", second_b, grad_upper_b, preferred_element_type=jnp.float32)
    grad_second = feed_back(
        jnp.einsum("rf,df->rd", grad_upper_b, w_up, preferred_element_type=jnp.float32)
    )
    grad_middle = grad_result + normalize_back(grad_second * gains[1], normed_two, inverse_two)
    grad_middle_b = grad_middle.astype(jnp.bfloat16)
    grad_wout = jnp.einsum("ri,ro->io", mixed_b, grad_middle_b, preferred_element_type=jnp.float32)
    grad_mixed = jnp.einsum("ro,io->ri", grad_middle_b, w_out, preferred_element_type=jnp.float32)
    grad_mixed_b = grad_mixed.astype(jnp.bfloat16).reshape(rows, local_heads, HEAD_DIM)
    grad_probs = jnp.einsum(
        "qhd,khd->hqk", grad_mixed_b, split[:, 2], preferred_element_type=jnp.float32
    )
    grad_values = jnp.einsum(
        "hqk,qhd->khd", probs_b, grad_mixed_b, preferred_element_type=jnp.float32
    )
    grad_scores = probs * (grad_probs - jnp.sum(probs * grad_probs, axis=-1, keepdims=True))
    grad_scores_b = grad_scores.astype(jnp.bfloat16)
    grad_queries = jnp.einsum(
        "hqk,khd->qhd", grad_scores_b, split[:, 1], preferred_element_type=jnp.float32
    ) * HEAD_DIM ** (-0.5)
    grad_keys = jnp.einsum(
        "hqk,qhd->khd", grad_scores_b, split[:, 0], preferred_element_type=jnp.float32
    ) * HEAD_DIM ** (-0.5)
    grad_packed = jnp.stack((grad_queries, grad_keys, grad_values), axis=1)
    grad_packed_b = grad_packed.reshape(rows, 3 * local_heads * HEAD_DIM).astype(jnp.bfloat16)
    grad_qkv = jnp.einsum("rd,re->de", first_b, grad_packed_b, preferred_element_type=jnp.float32)
    grad_first = attention_back(
        jnp.einsum("re,de->rd", grad_packed_b, w_qkv, preferred_element_type=jnp.float32)
    )
    grad_hidden = grad_middle + normalize_back(grad_first * gains[0], normed_one, inverse_one)
    grad_gains = jnp.stack(
        (jnp.sum(grad_first * normed_one, axis=0), jnp.sum(grad_second * normed_two, axis=0))
    )
    grad_biases = jnp.stack((jnp.sum(grad_first, axis=0), jnp.sum(grad_second, axis=0)))
    return (grad_hidden, (grad_qkv, grad_wout, grad_up, grad_down, grad_gains, grad_biases))


def per_device(inputs, cotangent, seg_counts, w_qkv, w_out, w_up, w_down, gains, biases):
    sections = lax.axis_size("section")
    section = lax.axis_index("section")
    rows = MB_SER * SEG
    width = inputs.shape[1]
    micro = inputs.shape[0] // rows
    ticks = micro + sections - 1
    pairs = 1
    feed_rows = inputs.reshape(micro, rows, width)
    back_rows = cotangent.reshape(micro, rows, width)
    count_rows = seg_counts.reshape(micro, MB_SER)
    params = (w_qkv[0], w_out[0], w_up[0], w_down[0], gains[0], biases[0])
    joins = (keep_local, keep_local, keep_local, keep_local)
    block_rows = pairs * rows
    zero_terms = tuple((jnp.zeros(weight.shape, jnp.float32) for weight in params))

    def forward_tick(tick, carry):
        arrived, kept, results = carry
        position = tick - section
        active = (position >= 0) & (position < micro)
        slot = jnp.clip(position, 0, micro - 1)
        source = jnp.where(section == 0, feed_rows[slot], arrived)
        allowed = allowed_pairs(count_rows[slot])
        result = lax.cond(
            active,
            lambda state: layer_forward(state, params, allowed, joins)[0],
            lambda state: jnp.zeros_like(state),
            source,
        )
        kept = jnp.where(active, lax.dynamic_update_slice_in_dim(kept, source[None], slot, 0), kept)
        results = jnp.where(
            active, lax.dynamic_update_slice_in_dim(results, result[None], slot, 0), results
        )
        arrived = from_behind(result, "section", 1)
        return (arrived, kept, results)

    empty_rows = jnp.zeros((block_rows, width), jnp.bfloat16)
    empty_store = jnp.zeros((micro, block_rows, width), jnp.bfloat16)
    _, kept, results = lax.fori_loop(0, ticks, forward_tick, (empty_rows, empty_store, empty_store))

    def backward_tick(tick, carry):
        arrived, totals, returned = carry
        position = tick - (sections - 1 - section)
        active = (position >= 0) & (position < micro)
        slot = jnp.clip(position, 0, micro - 1)
        upstream = jnp.where(section == sections - 1, back_rows[slot], arrived)
        allowed = allowed_pairs(count_rows[slot])
        layer_input = kept[slot]

        def run_layer(state):
            grad_hidden, terms = layer_backward(layer_input, state, params, allowed, joins)
            return (grad_hidden.astype(jnp.bfloat16), terms)

        def skip_layer(state):
            return (jnp.zeros_like(state), zero_terms)

        grad_hidden_b, terms = lax.cond(active, run_layer, skip_layer, upstream)
        totals = tuple((total + term for total, term in zip(totals, terms)))
        returned = jnp.where(
            active,
            lax.dynamic_update_slice_in_dim(returned, grad_hidden_b[None], slot, 0),
            returned,
        )
        arrived = from_behind(grad_hidden_b, "section", -1)
        return (arrived, totals, returned)

    _, totals, returned = lax.fori_loop(
        0, ticks, backward_tick, (empty_rows, zero_terms, empty_store)
    )
    shares = (
        lax.psum_scatter(totals[0][None], "dp", scatter_dimension=1, tiled=True),
        lax.psum_scatter(totals[1][None], "dp", scatter_dimension=2, tiled=True),
        lax.psum_scatter(totals[2][None], "dp", scatter_dimension=1, tiled=True),
        lax.psum_scatter(totals[3][None], "dp", scatter_dimension=2, tiled=True),
        lax.psum_scatter(totals[4][None], "dp", scatter_dimension=2, tiled=True),
        lax.psum_scatter(totals[5][None], "dp", scatter_dimension=2, tiled=True),
    )
    summed = (
        lax.psum(shares[0].astype(jnp.bfloat16), "rep").astype(jnp.float32),
        lax.psum(shares[1].astype(jnp.bfloat16), "rep").astype(jnp.float32),
        lax.psum(shares[2].astype(jnp.bfloat16), "rep").astype(jnp.float32),
        lax.psum(shares[3].astype(jnp.bfloat16), "rep").astype(jnp.float32),
        lax.psum(shares[4].astype(jnp.bfloat16), "rep").astype(jnp.float32),
        lax.psum(shares[5].astype(jnp.bfloat16), "rep").astype(jnp.float32),
    )
    layer_outputs = results.reshape(1, micro * rows, width)
    input_grads = returned.reshape(1, micro * rows, width)
    return (
        layer_outputs,
        input_grads,
        summed[0],
        summed[1],
        summed[2],
        summed[3],
        summed[4],
        summed[5],
    )


def solution(mesh):
    placed = (
        P(("dp", "rep"), None),
        P(("dp", "rep"), None),
        P(("dp", "rep")),
        P("section", None, None),
        P("section", None, None),
        P("section", None, None),
        P("section", None, None),
        P("section", None, None),
        P("section", None, None),
    )
    return jax.shard_map(
        per_device,
        mesh=mesh,
        in_specs=placed,
        out_specs=(
            P("section", ("dp", "rep"), None),
            P("section", ("dp", "rep"), None),
            P("section", "dp", None),
            P("section", None, "dp"),
            P("section", "dp", None),
            P("section", None, "dp"),
            P("section", None, "dp"),
            P("section", None, "dp"),
        ),
        check_vma=False,
    )
```

profile of v0, /device:TPU:0, one launch (start us, length us, event | category | flops | bytes accessed | tf_op | source)
XLA Modules:
  0.0 1205.0 jit_solution(18255057795434790949)
XLA Ops:
  9.5 80.4 %while.48 = (s32[]{:T(128)}, bf16[128,1024]{1,0:T(8,128)(2,1)S(1)}, bf16[2,128,1024]{2,1,0:T(8,128)(2,1)S(1)}, bf16[2,128,1024]{2,1,0:T(8,128)(2,1)}, s32[]{:T(1...) while((s32[]{:T(128)}, bf16[128,1024]{1,0:T(8,128)(2,1)S(1)}, ...), condition=%wide.region_9.10_spmd, body=%wide.region_0.9_spmd.sunk | while | flops 2222163456 | bytes 41540956 | solution.py:205
  10.7 22.2 %conditional.5 = (bf16[128,1024]{1,0:T(8,128)(2,1)}, bf16[1,128,1024]{2,1,0:T(8,128)(2,1)}) conditional(s32[]{:T(128)} %convert_element_type.348, () %tuple.146, (bf16[128,1024]{1,0:T(8,128)(2,1)S(1)}, f32[2,1024]{1,0:T(2,128)}, f32[2,1024]{1,0:T(2,128)}, bf16[1024,3072]{1,0:T(8,128)(2,1)}, s32[8,16]{1,0:T(8,128)S(1)}, ...), branch_computations={%region_1.1_spmd, %region_2.8_spmd} | conditional | flops 2221770240 | bytes 38262244 | solution.py:190
  12.5 3.9 fusion.1
  21.5 2.2 convolution_convert_fusion.1
  25.4 5.8 fusion.5
  37.2 22.2 %conditional.5 = (bf16[128,1024]{1,0:T(8,128)(2,1)}, bf16[1,128,1024]{2,1,0:T(8,128)(2,1)}) conditional(s32[]{:T(128)} %convert_element_type.348, () %tuple.146, (bf16[128,1024]{1,0:T(8,128)(2,1)S(1)}, f32[2,1024]{1,0:T(2,128)}, f32[2,1024]{1,0:T(2,128)}, bf16[1024,3072]{1,0:T(8,128)(2,1)}, s32[8,16]{1,0:T(8,128)S(1)}, ...), branch_computations={%region_1.1_spmd, %region_2.8_spmd} | conditional | flops 2221770240 | bytes 38262244 | solution.py:190
  39.0 3.9 fusion.1
  48.0 2.2 convolution_convert_fusion.1
  51.9 5.8 fusion.5
  59.4 1.8 collective-permute-start
  65.7 22.5 %collective-permute-start = (bf16[128,1024]{1,0:T(8,128)(2,1)}, bf16[128,1024]{1,0:T(8,128)(2,1)S(1)}, u32[]{:S(2)}, u32[]{:S(2)}) collective-permute-start(bf16[128,1024]{1,0:T(8,128)(2,1)} %get-tuple-element.1496), channel_id=1, source_target_pairs={{0,16},{1,17},{2,18},{3,19},{4,20},{5,21},{6,22},{7,23},{8,24},{9,... | collective-permute-start | bytes 786440 | tf_op jit(solution)/shard_map/while/body/eval_jaxpr/ppermute | solution.py:19
  91.5 296.8 %while.49 = (s32[]{:T(128)}, bf16[128,1024]{1,0:T(8,128)(2,1)}, f32[1024,3072]{1,0:T(8,128)}, f32[1024,1024]{1,0:T(8,128)}, f32[1024,2048]{1,0:T(8,128)}, /*inde...) while((s32[]{:T(128)}, bf16[128,1024]{1,0:T(8,128)(2,1)}, ...), condition=%wide.region_28.29_spmd.clone, body=%wide.region_10.28_spmd.clone.sunk | while | flops 6145549824 | bytes 265440848 | solution.py:233
  92.1 19.7 %conditional.6 = (bf16[128,1024]{1,0:T(8,128)(2,1)}, f32[1024,3072]{1,0:T(8,128)}, f32[1024,1024]{1,0:T(8,128)}, f32[1024,2048]{1,0:T(8,128)}, f32[2048,1024]{1,...) conditional(s32[]{:T(128)} %convert_element_type.349, () %tuple.150, ...), branch_computations={%region_11.11_spmd, %region_12.27_spmd} | conditional | flops 6128633344 | bytes 157386656 | solution.py:223
  92.1 6.1 broadcast_in_dim.241
  98.2 4.2 broadcast_in_dim.243
  102.4 4.3 broadcast_in_dim.244
  106.7 2.5 broadcast_in_dim.242
  113.1 12.1 %select_add_fusion.11 = f32[1024,3072]{1,0:T(8,128)} fusion(f32[1024,3072]{1,0:T(8,128)} %get-tuple-element.1520, f32[1024,3072]{1,0:T(8,128)} %get-tuple-element.1625, pred[]{:T(512)S(6)} %compare.3), kind=kLoop, calls=%fused_computation.175.clone.1 | loop fusion | flops 6291456 | bytes 37748736 | tf_op jit(solution)/shard_map/while/body/eval_jaxpr/add | solution.py:224
  125.2 9.4 select_add_fusion.13
  134.6 9.6 select_add_fusion.14
  144.2 5.6 select_add_fusion.12
  150.7 8.0 collective-permute-done.1
  160.0 64.2 %conditional.6 = (bf16[128,1024]{1,0:T(8,128)(2,1)}, f32[1024,3072]{1,0:T(8,128)}, f32[1024,1024]{1,0:T(8,128)}, f32[1024,2048]{1,0:T(8,128)}, f32[2048,1024]{1,...) conditional(s32[]{:T(128)} %convert_element_type.349, () %tuple.150, ...), branch_computations={%region_11.11_spmd, %region_12.27_spmd} | conditional | flops 6128633344 | bytes 157386656 | solution.py:223
  161.2 3.9 fusion.48
  177.7 3.7 fusion.128
  181.5 2.4 fusion.60
  183.9 4.6 fusion.116
  200.6 2.4 copy.75
  203.1 7.7 fusion.87
  210.8 2.4 fusion.75
  214.4 2.6 fusion.101
  217.1 4.5 fusion.81
  225.5 14.9 %select_add_fusion.11 = f32[1024,3072]{1,0:T(8,128)} fusion(f32[1024,3072]{1,0:T(8,128)} %get-tuple-element.1520, f32[1024,3072]{1,0:T(8,128)} %get-tuple-element.1625, pred[]{:T(512)S(6)} %compare.3), kind=kLoop, calls=%fused_computation.175.clone.1 | loop fusion | flops 6291456 | bytes 37748736 | tf_op jit(solution)/shard_map/while/body/eval_jaxpr/add | solution.py:224
  240.5 11.8 select_add_fusion.13
  252.3 12.0 select_add_fusion.14
  264.3 6.9 select_add_fusion.12
  274.4 64.2 %conditional.6 = (bf16[128,1024]{1,0:T(8,128)(2,1)}, f32[1024,3072]{1,0:T(8,128)}, f32[1024,1024]{1,0:T(8,128)}, f32[1024,2048]{1,0:T(8,128)}, f32[2048,1024]{1,...) conditional(s32[]{:T(128)} %convert_element_type.349, () %tuple.150, ...), branch_computations={%region_11.11_spmd, %region_12.27_spmd} | conditional | flops 6128633344 | bytes 157386656 | solution.py:223
  275.6 3.9 fusion.48
  292.2 3.7 fusion.128
  295.9 2.4 fusion.60
  298.3 4.6 fusion.116
  315.0 2.4 copy.75
  317.5 7.7 fusion.87
  325.3 2.4 fusion.75
  328.9 2.6 fusion.101
  331.5 4.5 fusion.81
  340.0 14.9 %select_add_fusion.11 = f32[1024,3072]{1,0:T(8,128)} fusion(f32[1024,3072]{1,0:T(8,128)} %get-tuple-element.1520, f32[1024,3072]{1,0:T(8,128)} %get-tuple-element.1625, pred[]{:T(512)S(6)} %compare.3), kind=kLoop, calls=%fused_computation.175.clone.1 | loop fusion | flops 6291456 | bytes 37748736 | tf_op jit(solution)/shard_map/while/body/eval_jaxpr/add | solution.py:224
  354.9 11.8 select_add_fusion.13
  366.7 12.0 select_add_fusion.14
  378.7 6.9 select_add_fusion.12
  392.7 86.8 %reduce-scatter.13.cloned.1.call-done = f32[1,1024,128]{2,1,0:T(8,128)} async-done(((f32[1,1024,1024]{2,1,0:T(8,128)}), f32[1,1024,128]{2,1,0:T(8,128)}) %reduce-scatter.13.cloned.1.call-update) | async-done | bytes 524304 | tf_op jit(solution)/shard_map/reduce_scatter | solution.py:238
  481.4 151.1 %reduce-scatter.15.cloned.1.call-done = f32[1,128,2048]{2,1,0:T(8,128)} async-done(((f32[1,1024,2048]{2,1,0:T(8,128)}), f32[1,128,2048]{2,1,0:T(8,128)}) %reduce-scatter.15.cloned.1.call-update) | async-done | bytes 1048592 | tf_op jit(solution)/shard_map/reduce_scatter | solution.py:239
  632.5 2.1 convert_element_type.224
  634.5 150.0 %reduce-scatter.17.cloned.1.call-done = f32[1,2048,128]{2,1,0:T(8,128)} async-done(((f32[1,2048,1024]{2,1,0:T(8,128)}), f32[1,2048,128]{2,1,0:T(8,128)}) %reduce-scatter.17.cloned.1.call-update) | async-done | bytes 1048592 | tf_op jit(solution)/shard_map/reduce_scatter | solution.py:240
  784.5 2.1 convert_element_type.226
  786.6 208.1 %reduce-scatter.11.cloned.1.call-done = f32[1,128,3072]{2,1,0:T(8,128)} async-done(((f32[1,1024,3072]{2,1,0:T(8,128)}), f32[1,128,3072]{2,1,0:T(8,128)}) %reduce-scatter.11.cloned.1.call-update) | async-done | bytes 1572880 | tf_op jit(solution)/shard_map/reduce_scatter | solution.py:237
  994.7 2.4 convert_element_type.220
  997.1 62.8 %reduce-scatter.19.cloned.1.call-done = f32[128,2]{1,0:T(8,128)} async-done(((f32[1024,2]{1,0:T(8,128)}), f32[128,2]{1,0:T(8,128)}) %reduce-scatter.19.cloned.1.call-update) | async-done | bytes 1040
  1060.9 63.2 %reduce-scatter.21.cloned.1.call-done = f32[128,2]{1,0:T(8,128)} async-done(((f32[1024,2]{1,0:T(8,128)}), f32[128,2]{1,0:T(8,128)}) %reduce-scatter.21.cloned.1.call-update) | async-done | bytes 1040
  1125.0 4.9 all-reduce
  1131.1 58.7 %all-reduce.4.cloned.1.call-done = (bf16[1,128,3072]{2,1,0:T(8,128)(2,1)}, bf16[1,1024,128]{2,1,0:T(8,128)(2,1)}, bf16[1,128,2048]{2,1,0:T(8,128)(2,1)}, bf16[1,2048,128]{2,1,0:T(8,128)(2,1)}) async-done(((bf16[1,128,3072]{2,1,0:T(8,128)(2,1)}, bf16[1,1024,128]{2,1,0:T(8,128)(2,1)}, bf16[1,128,2048]{2,1,0:T(8,128)(2,1)}, bf16[1,2048,128]{2,1,0:T(8,128)(2,1)}), (bf16[1,128,3072]{2,1,0:T(8,128)(2,1)}, ...) | async-done | bytes 2097168 | tf_op jit(solution)/shard_map/psum | solution.py:245
  1189.8 2.4 convert_element_type.221
  1192.2 2.1 convert_element_type.225
  1194.3 2.1 convert_element_type.227
  (340 shorter events, 122.5 us)
Async XLA Ops:
  7.2 472.4 %reduce-scatter.13.cloned.1.call-start = ((), (), s32[]{:S(2)}) async-start(), calls=%async_computation.7 | async-start | bytes 4718592 | tf_op jit(solution)/shard_map/reduce_scatter | solution.py:238
  12.5 4.9 copy-start.26
  16.4 7.3 copy-start
  18.3 7.2 copy-start.25
  32.9 3.1 collective-permute-start
  39.0 4.9 copy-start.26
  42.9 7.3 copy-start
  44.7 7.2 copy-start.25
  59.4 3.6 collective-permute-start
  65.7 24.3 %collective-permute-start = (bf16[128,1024]{1,0:T(8,128)(2,1)}, bf16[128,1024]{1,0:T(8,128)(2,1)S(1)}, u32[]{:S(2)}, u32[]{:S(2)}) collective-permute-start(bf16[128,1024]{1,0:T(8,128)(2,1)} %get-tuple-element.1496), channel_id=1, source_target_pairs={{0,16},{1,17},{2,18},{3,19},{4,20},{5,21},{6,22},{7,23},{8,24},{9,... | collective-permute-start | bytes 786440 | tf_op jit(solution)/shard_map/while/body/eval_jaxpr/ppermute | solution.py:19
  111.8 46.9 %collective-permute-start.1 = (bf16[128,1024]{1,0:T(8,128)(2,1)}, bf16[128,1024]{1,0:T(8,128)(2,1)S(1)}, u32[]{:S(2)}, u32[]{:S(2)}) collective-permute-start(bf16[128,1024]{1,0:T(8,128)(2,1)} %get-tuple-element.1519), channel_id=1, source_target_pairs={{16,0},{17,1},{18,2},{19,3},{20,4},{21,5},{22,6},{23,7},{24,8},{25... | collective-permute-start | bytes 786440 | tf_op jit(solution)/shard_map/while/body/eval_jaxpr/ppermute | solution.py:19
  144.2 5.6 copy-start.19
  144.2 5.6 copy-start.22
  144.2 6.4 copy-start.12
  150.6 8.2 copy-start.20
  150.6 8.2 copy-start.23
  150.7 8.1 copy-start.13
  160.0 5.5 copy-start.14
  160.2 5.1 copy-start.15
  160.4 4.9 copy-start.17
  161.2 4.3 copy-start.27
  165.1 10.3 copy-start.1
  165.5 7.4 copy-start.7
  165.5 16.0 %copy-start.8 = (bf16[128,1,8,128]{3,2,1,0:T(8,128)(2,1)}, bf16[128,1,8,128]{3,2,1,0:T(8,128)(2,1)S(1)}, u32[]{:S(2)}) copy-start(bf16[128,1,8,128]{3,2,1,0:T(8,128)(2,1)S(1)} %get-tuple-element.1274) | copy-start | bytes 786436 | tf_op jit(solution)/shard_map/while/body/eval_jaxpr/cond
  175.4 6.1 copy-start.5
  175.4 6.1 copy-start.3
  192.0 11.1 copy-start.16
  192.0 11.1 copy-start.18
  200.6 10.2 slice-start
  203.1 7.7 slice-start.1
  203.1 7.7 copy-start.2
  210.8 3.6 copy-start.6
  210.8 6.2 copy-start.4
  224.2 48.7 %collective-permute-start.1 = (bf16[128,1024]{1,0:T(8,128)(2,1)}, bf16[128,1024]{1,0:T(8,128)(2,1)S(1)}, u32[]{:S(2)}, u32[]{:S(2)}) collective-permute-start(bf16[128,1024]{1,0:T(8,128)(2,1)} %get-tuple-element.1519), channel_id=1, source_target_pairs={{16,0},{17,1},{18,2},{19,3},{20,4},{21,5},{22,6},{23,7},{24,8},{25... | collective-permute-start | bytes 786440 | tf_op jit(solution)/shard_map/while/body/eval_jaxpr/ppermute | solution.py:19
  264.3 6.9 copy-start.19
  264.3 6.9 copy-start.22
  264.3 7.6 copy-start.12
  274.4 5.5 copy-start.14
  274.6 5.2 copy-start.15
  274.8 4.9 copy-start.17
  275.6 4.3 copy-start.27
  279.5 10.3 copy-start.1
  279.9 7.4 copy-start.7
  279.9 16.0 %copy-start.8 = (bf16[128,1,8,128]{3,2,1,0:T(8,128)(2,1)}, bf16[128,1,8,128]{3,2,1,0:T(8,128)(2,1)S(1)}, u32[]{:S(2)}) copy-start(bf16[128,1,8,128]{3,2,1,0:T(8,128)(2,1)S(1)} %get-tuple-element.1274) | copy-start | bytes 786436 | tf_op jit(solution)/shard_map/while/body/eval_jaxpr/cond
  289.8 6.1 copy-start.5
  289.8 6.1 copy-start.3
  306.4 11.1 copy-start.16
  306.4 11.1 copy-start.18
  315.0 10.2 slice-start
  317.5 7.7 slice-start.1
  317.5 7.7 copy-start.2
  325.2 3.6 copy-start.6
  325.3 6.2 copy-start.4
  338.7 48.7 %collective-permute-start.1 = (bf16[128,1024]{1,0:T(8,128)(2,1)}, bf16[128,1024]{1,0:T(8,128)(2,1)S(1)}, u32[]{:S(2)}, u32[]{:S(2)}) collective-permute-start(bf16[128,1024]{1,0:T(8,128)(2,1)} %get-tuple-element.1519), channel_id=1, source_target_pairs={{16,0},{17,1},{18,2},{19,3},{20,4},{21,5},{22,6},{23,7},{24,8},{25... | collective-permute-start | bytes 786440 | tf_op jit(solution)/shard_map/while/body/eval_jaxpr/ppermute | solution.py:19
  378.7 6.9 copy-start.19
  378.7 6.9 copy-start.22
  378.7 7.6 copy-start.12
  388.3 244.2 %reduce-scatter.15.cloned.1.call-start = ((), (), s32[]{:S(2)}) async-start(), calls=%async_computation.8 | async-start | bytes 9437184 | tf_op jit(solution)/shard_map/reduce_scatter | solution.py:239
  389.0 395.5 %reduce-scatter.17.cloned.1.call-start = ((), (), s32[]{:S(2)}) async-start(), calls=%async_computation.9 | async-start | bytes 9437184 | tf_op jit(solution)/shard_map/reduce_scatter | solution.py:240
  389.8 605.0 %reduce-scatter.11.cloned.1.call-start = ((), (), s32[]{:S(2)}) async-start(), calls=%async_computation.6 | async-start | bytes 14155776 | tf_op jit(solution)/shard_map/reduce_scatter | solution.py:237
  389.8 1.8 copy-start.24
  390.3 669.6 %reduce-scatter.19.cloned.1.call-start = ((), (), s32[]{:S(2)}) async-start(), calls=%async_computation.10 | async-start | bytes 589824
  391.6 732.6 %reduce-scatter.21.cloned.1.call-start = ((), (), s32[]{:S(2)}) async-start(), calls=%async_computation.11 | async-start | bytes 589824
  392.7 797.1 %all-reduce.4.cloned.1.call-start = ((), (), s32[]{:S(2)}) async-start(), calls=%async_computation.12 | async-start | bytes 4194304 | tf_op jit(solution)/shard_map/psum | solution.py:245
  (14 other events, 12.3 us)
Sparse Core Ops, SparseCore 0:
  388.4 91.1 reduce-scatter.12
  483.6 148.7 reduce-scatter.14
  636.1 148.3 reduce-scatter.16
  788.4 206.2 reduce-scatter.10
  998.9 61.0 reduce-scatter.18
  1063.2 60.8 reduce-scatter.20
  1127.3 62.4 all-reduce.3
where the time goes:
time: 1210 us
  waiting for transfers between devices  791 us (65%)
  other arithmetic  180 us (15%)
  matrix products  115 us (10%)
  local copies, waits for them, and re-layouts  68.8 us (6%)
  starting transfers between devices  29.8 us (2%)
  between operations  14.2 us (1%)
    reduce_scatter x1, waiting for transfers between devices, per_device(): lax.psum_scatter(totals[0][None], 'dp', scatter_dimension=1, tiled=True)  208 us
    reduce_scatter x1, waiting for transfers between devices, per_device(): lax.psum_scatter(totals[2][None], 'dp', scatter_dimension=1, tiled=True)  151 us
    reduce_scatter x1, waiting for transfers between devices, per_device(): lax.psum_scatter(totals[3][None], 'dp', scatter_dimension=2, tiled=True)  150 us
    add x15, other arithmetic, backward_tick(): totals = tuple((total + term for total, term in zip(totals, terms)))  130 us
    unnamed x9, waiting for transfers between devices  128 us
    reduce_scatter x1, waiting for transfers between devices, per_device(): lax.psum_scatter(totals[1][None], 'dp', scatter_dimension=2, tiled=True)  86.8 us
    psum x1, waiting for transfers between devices, per_device(): lax.psum(shares[0].astype(jnp.bfloat16), 'rep').astype(jnp.float32)  58.7 us
    ppermute x6, starting transfers between devices, from_behind(): return lax.ppermute(block, axis, route)  29.5 us
  transfers between devices with their start and end apart: 13, of which 8 were waited for; matrix products, arithmetic and copies ran while one was open for 13% of the time, Pallas kernels for 0%

commit v1 on v0

v1 whole, which is shorter than its diff:
```python
from functools import partial

import jax
import jax.numpy as jnp
from jax import lax
from jax.sharding import PartitionSpec as P

SEG = 16
HEAD_DIM = 128
BLOCK = 128
epsilon = 1e-05
f32 = jnp.float32
bf16 = jnp.bfloat16


def normalize(hidden):
    average = jnp.mean(hidden, axis=-1, keepdims=True)
    centred = hidden - average
    inverse = lax.rsqrt(jnp.mean(centred * centred, axis=-1, keepdims=True) + epsilon)
    return (centred * inverse, inverse)


def normalize_back(grad_normed, normed, inverse):
    centre_term = jnp.mean(grad_normed, axis=-1, keepdims=True)
    slope_term = normed * jnp.mean(grad_normed * normed, axis=-1, keepdims=True)
    return inverse * (grad_normed - centre_term - slope_term)


def allowed_pairs(counts):
    rows = counts.shape[0] * SEG
    blocks = rows // BLOCK
    ids = jnp.arange(rows, dtype=jnp.int32).reshape(blocks, BLOCK)
    first = jnp.repeat(SEG - counts, SEG).reshape(blocks, BLOCK)
    position = ids % SEG
    owner = ids // SEG
    same = owner[:, :, None] == owner[:, None, :]
    causal = position[:, None, :] <= position[:, :, None]
    valid = (position >= first)[:, None, :] | (ids[:, :, None] == ids[:, None, :])
    return same & causal & valid


def forward(hidden_b, params, allowed):
    w_qkv, w_out, w_up, w_down, gains, biases = params
    rows = hidden_b.shape[0]
    heads = w_qkv.shape[1] // (3 * HEAD_DIM)
    hidden = hidden_b.astype(f32)
    n1, i1 = normalize(hidden)
    a = (n1 * gains[0] + biases[0]).astype(bf16)
    packed = jnp.dot(a, w_qkv, preferred_element_type=f32).astype(bf16)
    split = packed.reshape(rows // BLOCK, BLOCK, 3, heads, HEAD_DIM)
    scores = jnp.einsum("bqhd,bkhd->bhqk", split[:, :, 0], split[:, :, 1], preferred_element_type=f32)
    scores = jnp.where(allowed[:, None], scores * HEAD_DIM**-0.5, -1e30)
    raised = jnp.exp(scores - jnp.max(scores, axis=-1, keepdims=True))
    probs = raised / jnp.sum(raised, axis=-1, keepdims=True)
    probs_b = probs.astype(bf16)
    mixed = jnp.einsum("bhqk,bkhd->bqhd", probs_b, split[:, :, 2], preferred_element_type=f32)
    mixed_b = mixed.reshape(rows, heads * HEAD_DIM).astype(bf16)
    middle = hidden + jnp.dot(mixed_b, w_out, preferred_element_type=f32)
    n2, i2 = normalize(middle)
    c = (n2 * gains[1] + biases[1]).astype(bf16)
    upper = jnp.dot(c, w_up, preferred_element_type=f32)
    g = jax.nn.gelu(upper, approximate=True).astype(bf16)
    result = (middle + jnp.dot(g, w_down, preferred_element_type=f32)).astype(bf16)
    return result, (n1, i1, a, split, probs, probs_b, mixed_b, n2, i2, c, upper, g)


def backward(saved, grad_b, params):
    w_qkv, w_out, w_up, w_down, gains, biases = params
    n1, i1, a, split, probs, probs_b, mixed_b, n2, i2, c, upper, g = saved
    rows = grad_b.shape[0]
    heads = w_qkv.shape[1] // (3 * HEAD_DIM)
    d_g = jnp.einsum("rd,fd->rf", grad_b, w_down, preferred_element_type=f32)
    d_u = jax.vjp(partial(jax.nn.gelu, approximate=True), upper)[1](d_g)[0].astype(bf16)
    d_c = jnp.einsum("rf,df->rd", d_u, w_up, preferred_element_type=f32)
    d_m = grad_b.astype(f32) + normalize_back(d_c * gains[1], n2, i2)
    d_mb = d_m.astype(bf16)
    d_o = jnp.einsum("ro,io->ri", d_mb, w_out, preferred_element_type=f32).astype(bf16)
    d_o = d_o.reshape(rows // BLOCK, BLOCK, heads, HEAD_DIM)
    d_probs = jnp.einsum("bqhd,bkhd->bhqk", d_o, split[:, :, 2], preferred_element_type=f32)
    d_v = jnp.einsum("bhqk,bqhd->bkhd", probs_b, d_o, preferred_element_type=f32)
    d_s = (probs * (d_probs - jnp.sum(probs * d_probs, axis=-1, keepdims=True))).astype(bf16)
    d_q = jnp.einsum("bhqk,bkhd->bqhd", d_s, split[:, :, 1], preferred_element_type=f32) * HEAD_DIM**-0.5
    d_k = jnp.einsum("bhqk,bqhd->bkhd", d_s, split[:, :, 0], preferred_element_type=f32) * HEAD_DIM**-0.5
    d_p = jnp.stack((d_q, d_k, d_v), axis=2).reshape(rows, -1).astype(bf16)
    d_a = jnp.einsum("re,de->rd", d_p, w_qkv, preferred_element_type=f32)
    d_h = (d_m + normalize_back(d_a * gains[0], n1, i1)).astype(bf16)
    return d_h, (d_u, d_mb, d_p, d_a, d_c)


def per_device(inputs, cotangent, seg_counts, w_qkv, w_out, w_up, w_down, gains, biases):
    last = lax.axis_size("section") - 1
    section = lax.axis_index("section")
    params = (w_qkv[0], w_out[0], w_up[0], w_down[0], gains[0], biases[0])
    allowed = allowed_pairs(seg_counts)
    sent = forward(inputs, params, allowed)[0]
    hidden = jnp.where(section == 0, inputs, lax.ppermute(sent, "section", [(0, 1)]))
    result, saved = forward(hidden, params, allowed)
    sent = backward(saved, cotangent, params)[0]
    grad = jnp.where(section == last, cotangent, lax.ppermute(sent, "section", [(1, 0)]))
    d_h, (d_u, d_mb, d_p, d_a, d_c) = backward(saved, grad, params)
    n1, i1, a, split, probs, probs_b, mixed_b, n2, i2, c, upper, g = saved

    def outer(left, right):
        return jnp.einsum("ri,ro->io", left, right, preferred_element_type=f32).astype(bf16)[None]

    terms = (outer(a, d_p), outer(mixed_b, d_mb), outer(c, d_u), outer(g, grad))
    small_g = jnp.stack((jnp.sum(d_a * n1, axis=0), jnp.sum(d_c * n2, axis=0)))[None]
    small_b = jnp.stack((jnp.sum(d_a, axis=0), jnp.sum(d_c, axis=0)))[None]
    terms = terms + (small_g, small_b)
    dims = (1, 2, 1, 2, 2, 2)
    shares = [
        lax.psum_scatter(term, "dp", scatter_dimension=dim, tiled=True) for term, dim in zip(terms, dims)
    ]
    summed = [lax.psum(share.astype(bf16), "rep").astype(f32) for share in shares]
    return (result[None], d_h[None], *summed)


def solution(mesh):
    rows = P(("dp", "rep"), None)
    layer = P("section", None, None)
    return jax.shard_map(
        per_device,
        mesh=mesh,
        in_specs=(rows, rows, P(("dp", "rep"))) + (layer,) * 6,
        out_specs=(
            P("section", ("dp", "rep"), None),
            P("section", ("dp", "rep"), None),
            P("section", "dp", None),
            P("section", None, "dp"),
            P("section", "dp", None),
            P("section", None, "dp"),
            P("section", None, "dp"),
            P("section", None, "dp"),
        ),
        check_vma=False,
    )
```

time: 1210 us -> 725 us (0.60)
  waiting for transfers between devices: 791 us -> 477 us
  other arithmetic: 180 us -> 31.2 us
  starting transfers between devices: 29.8 us -> 4.41 us
  local copies, waits for them, and re-layouts: 68.8 us -> 90 us
  matrix products: 115 us -> 94.3 us
    reduce_scatter x4 -> x2, waiting for transfers between devices: 596 us -> 207 us  [per_device(): lax.psum_scatter(term, 'dp', scatter_dimension=dim, tiled=True)]
    add x17 -> x1, other arithmetic: 131 us -> 1.67 us  [backward(): d_m = grad_b.astype(f32) + normalize_back(d_c * gains[1], n2, i2)]
    unnamed x9 -> x11, waiting for transfers between devices: 128 us -> 207 us
    unnamed x8 -> x76, local copies, waits for them, and re-layouts: 4 us -> 68.5 us
    ppermute x6 -> x2, starting transfers between devices: 29.5 us -> 3.91 us  [the longest x1 2.63 us: per_device(): lax.ppermute(sent, 'section', [(0, 1)])]
    broadcast_in_dim x21 -> x3, local copies, waits for them, and re-layouts: 22.1 us -> 0.24 us  [allowed_pairs(): first = jnp.repeat(SEG - counts, SEG).reshape(blocks, BLOCK)]
    dot_general x44 -> x30, matrix products: 115 us -> 94.3 us  [the longest x4 18.5 us: outer(): jnp.einsum('ri,ro->io', left, right, preferred_element_type=f32)]
    convert_element_type x16 -> x10, other arithmetic: 24 us -> 9.61 us  [the longest x6 7.57 us: per_device(): lax.psum(share.astype(bf16), 'rep').astype(f32)]
  transfers between devices with their start and end apart: 13 -> 9, of which waited for: 8 -> 8; matrix products, arithmetic and copies ran while one was open for 13% -> 12% of each run, Pallas kernels for 0% -> 0%
where the time goes in v1:
time: 725 us; the launch traced here: 717 us
  waiting for transfers between devices  477 us (66%)
  matrix products  94.3 us (13%)
  local copies, waits for them, and re-layouts  90 us (12%)
  other arithmetic  31.2 us (4%)
  between operations  15.1 us (2%)
    unnamed x11, waiting for transfers between devices  207 us
    reduce_scatter x2, waiting for transfers between devices, per_device(): lax.psum_scatter(term, 'dp', scatter_dimension=dim, tiled=True)  207 us
    unnamed x76, local copies, waits for them, and re-layouts  68.5 us
    psum x1, waiting for transfers between devices, per_device(): lax.psum(share.astype(bf16), 'rep').astype(f32)  58.6 us
    dot_general x4, matrix products, outer(): jnp.einsum('ri,ro->io', left, right, preferred_element_type=f32)  18.5 us
  transfers between devices with their start and end apart: 9, of which 8 were waited for; matrix products, arithmetic and copies ran while one was open for 12% of the time, Pallas kernels for 0%

profile of v1, /device:TPU:0, one launch (start us, length us, event | category | flops | bytes accessed | tf_op | source)
XLA Modules:
  0.0 717.0 jit_solution(17454511011516978575)
XLA Ops:
  8.1 1.2 convert_reduce_fusion.1
  9.3 1.3 fusion.142
  12.4 4.9 fusion.63
  20.2 2.9 fusion.125
  23.1 1.3 copy.85
  26.4 7.5 %fusion.93 = bf16[256,1024]{1,0:T(8,128)(2,1)} fusion(f32[256,1024]{1,0:T(8,128)} %copy-done.15, bf16[1,2048,1024]{2,1,0:T(8,128)(2,1)} %param.15, bf16[1,1024,2048]{2,1,0:T(8,128)(2,1)} %param.14, f32[1024]{0:T(1024)S(1)} %bitcast.290, f32[1024]{0:T(1024)S(1)} %bitcast.281, f32[256]{0:T(256)S(1)} %add_rsqrt_fusion.2, f32[256]{0:T(256)S(1)} %broadcast_multiply_fusion.10), kind=kOutput, calls=%fused_computation.92 | convolution fusion | flops 2154037248 | bytes 9971712 | tf_op jit(solution)/shard_map/dot_general | solution.py:63
  33.9 2.6 collective-permute-start
  36.6 1.4 collective-permute-done
  38.5 4.7 fusion.60
  43.6 1.1 fusion.199
  44.7 2.5 copy.148
  48.6 1.2 fusion.205
  49.8 2.2 fusion.126
  52.0 1.1 copy.90
  53.1 2.1 fusion.206
  55.6 2.7 fusion.22
  58.3 8.4 %fusion.198 = (f32[256]{0:T(256)S(1)}, f32[256]{0:T(256)S(1)}, f32[256,1024]{1,0:T(8,128)}) fusion(f32[256]{0:T(256)S(1)} %add_rsqrt_fusion, f32[256,1024]{1,0:T(8,128)S(1)} %get-tuple-element.43, f32[256]{0:T(256)S(1)} %broadcast_multiply_fusion.8, f32[1024]{0:T(1024)S(1)} %bitcast.283, bf16[1,1024,2048]{2,1,0:T(8,128)(2,1)} %param.14, ...), kind=kOutput, calls=%fused_computation.231 | convolution fusion | flops 2159541760 | bytes 13115392 | tf_op jit(solution)/shard_map/rf,df->rd/dot_general | solution.py:74
  66.7 2.2 fusion.119
  69.8 2.1 copy.99
  72.0 3.0 fusion.127
  74.9 2.0 multiply_reduce_fusion.3
  79.1 11.6 %pad_maximum_fusion = bf16[2,128,3,8,128]{4,1,3,0,2:T(8,128)(2,1)S(1)} fusion(bf16[2,128,1,8,128]{4,1,3,0,2:T(8,128)(2,1)S(1)} %copy-done.25, bf16[2,128,1,8,128]{4,1,3,0,2:T(8,128)(2,1)S(1)} %fusion.114, bf16[2,128,1,8,128]{4,1,3,0,2:T(8,128)(2,1)S(1)} %fusion.115), kind=kLoop, calls=%fused_computation.63 | loop fusion | flops 1572864 | bytes 3145728 | tf_op jit(solution)/shard_map/stack | solution.py:84
  90.7 2.2 copy.102
  92.8 3.7 convert_element_type.182
  96.6 5.4 fusion.197
  102.1 1.5 fusion.134
  103.5 1.3 collective-permute-start.1
  104.8 2.8 collective-permute-done.1
  107.7 1.1 broadcast_select_fusion
  108.8 5.4 add_convert_fusion
  114.2 1.6 multiply_reduce_fusion
  115.9 1.7 multiply_add_fusion
  117.6 2.1 convert_bitcast_fusion.3
  119.6 10.8 %copy.135 = bf16[1,1024,1024]{1,0,2:T(2,128)(2,1)} copy(bf16[1,1024,1024]{2,1,0:T(8,128)(2,1)} %convert_bitcast_fusion.3) | data formatting | bytes 4194304
  130.5 4.3 copy.188
  134.8 5.3 convert_bitcast_fusion.1
  140.1 20.6 %copy.137 = bf16[1,2048,1024]{1,0,2:T(2,128)(2,1)} copy(bf16[1,2048,1024]{2,1,0:T(8,128)(2,1)} %convert_bitcast_fusion.1) | data formatting | bytes 8388608
  160.7 8.0 %copy.187 = bf16[1024,1,2048]{2,0,1:T(8,128)(2,1)} copy(bf16[1024,1,2048]{2,1,0:T(2,128)(2,1)} %bitcast.260) | data formatting | bytes 8388608
  168.8 5.0 convert_bitcast_fusion.2
  175.7 2.1 copy.111
  177.8 3.1 convolution_bitcast_fusion
  180.9 2.0 multiply_reduce_fusion.1
  185.2 2.2 copy.114
  187.4 3.7 convert_element_type.190
  191.1 6.2 convert_bitcast_fusion
  197.4 6.4 fusion.140
  203.8 1.0 copy.141
  204.9 1.0 copy.139
  206.0 2.0 reshape_bitcast_fusion.1
  208.0 1.9 copy.136
  209.9 85.5 %reduce-scatter.21.cloned.1.call-done = bf16[128,2048]{1,0:T(8,128)(2,1)} async-done(((bf16[1024,2048]{1,0:T(8,128)(2,1)}), bf16[128,2048]{1,0:T(8,128)(2,1)}) %reduce-scatter.21.cloned.1.call-update) | async-done | bytes 524304
  295.4 2.6 reshape_bitcast_fusion
  298.1 3.5 copy.138
  301.6 85.6 %reduce-scatter.17.cloned.1.call-done = bf16[1,128,2048]{2,1,0:T(8,128)(2,1)} async-done(((bf16[1,1024,2048]{2,1,0:T(8,128)(2,1)}), bf16[1,128,2048]{2,1,0:T(8,128)(2,1)}) %reduce-scatter.17.cloned.1.call-update) | async-done | bytes 524304 | tf_op jit(solution)/shard_map/reduce_scatter | solution.py:112
  387.2 121.2 %reduce-scatter.15.cloned.1.call-done = bf16[1,128,3072]{2,1,0:T(8,128)(2,1)} async-done(((bf16[1,1024,3072]{2,1,0:T(8,128)(2,1)}), bf16[1,128,3072]{2,1,0:T(8,128)(2,1)}) %reduce-scatter.15.cloned.1.call-update) | async-done | bytes 786448 | tf_op jit(solution)/shard_map/reduce_scatter | solution.py:112
  508.5 5.5 fusion.122
  513.9 1.2 fusion.151
  515.2 57.5 %reduce-scatter.25.cloned.1.call-done = f32[128,2]{1,0:T(8,128)} async-done(((f32[1024,2]{1,0:T(8,128)}), f32[128,2]{1,0:T(8,128)}) %reduce-scatter.25.cloned.1.call-update) | async-done | bytes 1040
  573.6 64.2 %reduce-scatter.23.cloned.1.call-done = f32[128,2]{1,0:T(8,128)} async-done(((f32[1024,2]{1,0:T(8,128)}), f32[128,2]{1,0:T(8,128)}) %reduce-scatter.23.cloned.1.call-update) | async-done | bytes 1040
  638.7 4.9 all-reduce
  644.7 58.6 %all-reduce.4.cloned.1.call-done = (bf16[1,128,3072]{2,1,0:T(8,128)(2,1)}, bf16[1,1024,128]{2,1,0:T(8,128)(2,1)}, bf16[1,128,2048]{2,1,0:T(8,128)(2,1)}, bf16[1,2048,128]{2,1,0:T(8,128)(2,1)}) async-done(((bf16[1,128,3072]{2,1,0:T(8,128)(2,1)}, bf16[1,1024,128]{2,1,0:T(8,128)(2,1)}, bf16[1,128,2048]{2,1,0:T(8,128)(2,1)}, bf16[1,2048,128]{2,1,0:T(8,128)(2,1)}), (bf16[1,128,3072]{2,1,0:T(8,128)(2,1)}, ...) | async-done | bytes 2097168 | tf_op jit(solution)/shard_map/psum | solution.py:114
  703.3 1.8 convert_element_type.195
  705.1 2.5 convert_element_type.193
  707.6 1.1 convert_element_type.197
  (128 shorter events, 21.7 us)
Async XLA Ops:
  7.2 17.2 %copy-start = (bf16[1,1024,1024]{2,1,0:T(8,128)(2,1)S(1)}, bf16[1,1024,1024]{2,1,0:T(8,128)(2,1)}, u32[]{:S(2)}) copy-start(bf16[1,1024,1024]{2,1,0:T(8,128)(2,1)} %param.13) | copy-start | bytes 6291460
  7.2 198.8 %reduce-scatter.19.cloned.1.call-start = ((), (), s32[]{:S(2)}) async-start(), calls=%async_computation.8 | async-start | bytes 2359296
  18.6 1.0 copy-start.20
  20.2 4.2 copy-start.7
  25.2 1.0 copy-start.15
  33.9 4.1 collective-permute-start
  38.2 5.1 copy-start.2
  44.7 5.1 copy-start.9
  44.7 5.1 copy-start.12
  47.6 1.0 copy-start.19
  53.1 2.5 copy-start.26
  55.2 59.0 %copy-start.1 = (f32[256,1024]{1,0:T(8,128)}, f32[256,1024]{1,0:T(8,128)S(1)}, u32[]{:S(2)}) copy-start(f32[256,1024]{1,0:T(8,128)S(1)} %get-tuple-element.43) | copy-start | bytes 3145732
  74.9 2.0 copy-start.5
  76.9 1.0 copy-start.10
  77.0 1.3 copy-start.13
  78.0 1.1 copy-start.25
  96.6 5.5 copy-start.3
  96.6 5.5 copy-start.16
  96.6 5.5 copy-start.21
  103.5 4.1 collective-permute-start.1
  108.8 7.1 copy-start.17
  108.8 5.4 copy-start.27
  114.2 1.6 copy-start.28
  115.8 1.7 copy-start.8
  134.8 160.7 %reduce-scatter.21.cloned.1.call-start = ((), (), s32[]{:S(2)}) async-start(), calls=%async_computation.9 | async-start | bytes 4718592
  168.8 218.4 %reduce-scatter.17.cloned.1.call-start = ((), (), s32[]{:S(2)}) async-start(), calls=%async_computation.7 | async-start | bytes 4718592 | tf_op jit(solution)/shard_map/reduce_scatter | solution.py:112
  173.8 334.6 %reduce-scatter.15.cloned.1.call-start = ((), (), s32[]{:S(2)}) async-start(), calls=%async_computation.6 | async-start | bytes 7077888 | tf_op jit(solution)/shard_map/reduce_scatter | solution.py:112
  180.9 2.0 copy-start.6
  182.9 1.1 copy-start.14
  182.9 1.4 copy-start.11
  184.0 1.1 copy-start.24
  197.3 375.4 %reduce-scatter.25.cloned.1.call-start = ((), (), s32[]{:S(2)}) async-start(), calls=%async_computation.11 | async-start | bytes 589824
  204.8 432.9 %reduce-scatter.23.cloned.1.call-start = ((), (), s32[]{:S(2)}) async-start(), calls=%async_computation.10 | async-start | bytes 589824
  206.0 497.3 %all-reduce.4.cloned.1.call-start = ((), (), s32[]{:S(2)}) async-start(), calls=%async_computation.12 | async-start | bytes 4194304 | tf_op jit(solution)/shard_map/psum | solution.py:114
  508.4 5.5 copy-start.4
  508.4 5.5 copy-start.18
  703.3 4.3 copy-start.23
  705.1 3.6 copy-start.22
Sparse Core Ops, SparseCore 0:
  134.9 69.7 reduce-scatter.18
  208.3 87.0 reduce-scatter.20
  299.5 87.6 reduce-scatter.16
  390.6 117.7 reduce-scatter.14
  511.6 61.0 reduce-scatter.24
  576.8 60.8 reduce-scatter.22
  640.8 62.4 all-reduce.3
